TPU v7x, 512 devices: a whole 4x8x8 slice. The times are simulated.
512 devices in a mesh: row: 16 (over z_hi, x, core), col: 32 (over y, z_lo).
Axes of the slice: x: 4, y: 8, z: 8 (z_hi: 2, z_lo: 4; z = z_hi * 4 + z_lo), core: 2. Of those that a mesh axis runs over, the one named last changes fastest.
Arguments:
- trunk: bfloat16 [4096, 512], P('row', 'col'), may hold values from -6 to 6
- proj_weight: bfloat16 [512, 128], P('col'), may hold values from -0.25 to 0.25
- conv_kernel: bfloat16 [9, 64, 64], replicated, may hold values from -0.25 to 0.25
- norm_gain: float32 [64], replicated, may hold values from 0.1 to 1.9
- norm_bias: float32 [64], replicated, may hold values from -3 to 3
Outputs:
- contact_map: bfloat16 [4096, 64, 4096], P('row', None, 'col')
All inputs are finite; a program needn't handle non-finite values.
Results may differ from a plain program's by a relative error of at most 0.0095.
Values may be sent and summed in bfloat16 or wider, within the bound.
No kernel may reach another device: no remote copies, remote signals or barrier semaphores. Data moves between devices by JAX's collectives and lax.ppermute only.
A program may use at most 128 MiB of HBM per device.

v0:
```python
import jax
import jax.numpy as jnp
from jax import lax
from jax.sharding import PartitionSpec as P

CONV_DILATION = 4


def pair_features(rows, cols, width):
    row_u = rows[:, :width].astype(jnp.float32)
    row_v = rows[:, width:].astype(jnp.float32)
    col_u = cols[:, :width].astype(jnp.float32).T
    col_v = cols[:, width:].astype(jnp.float32).T
    pair_block = row_u[:, :, None] * col_u[None] + row_v[:, :, None] + col_v[None]
    return pair_block.astype(jnp.bfloat16)


def inside_mask(first_entry, count_total, total_bins):
    position_index = (
        first_entry - CONV_DILATION + jnp.arange(count_total + 2 * CONV_DILATION, dtype=jnp.int32)
    )
    return ((position_index >= 0) & (position_index < total_bins)).astype(jnp.bfloat16)


def symmetric_conv(active, conv_kernel):
    width = conv_kernel.shape[1]
    grid = conv_kernel.reshape(3, 3, width, width).transpose(2, 3, 0, 1)
    stacked = jnp.concatenate([grid, grid.transpose(0, 1, 3, 2)], 0)
    result = lax.conv_general_dilated(
        active[None],
        stacked,
        (1, 1),
        "VALID",
        rhs_dilation=(CONV_DILATION, CONV_DILATION),
        dimension_numbers=("NHCW", "OIHW", "NHCW"),
        preferred_element_type=jnp.float32,
    )[0]
    return 0.5 * (result[:, :width] + result[:, width:])


def per_device(trunk, proj_weight, conv_kernel, norm_gain, norm_bias):
    block_rows = trunk.shape[0]
    width = norm_gain.shape[0]
    total_bins = block_rows * lax.axis_size("row")
    block_columns = total_bins // lax.axis_size("col")
    row_begin = lax.axis_index("row") * block_rows
    column_begin = lax.axis_index("col") * block_columns
    partial_sum = jnp.dot(trunk, proj_weight, preferred_element_type=jnp.float32)
    summed = lax.psum(partial_sum, "col").astype(jnp.bfloat16)
    feature_rows = lax.all_gather(summed, "row", axis=0, tiled=True)
    padded_map = jnp.pad(feature_rows, ((CONV_DILATION, CONV_DILATION), (0, 0)))
    widened_rows = lax.dynamic_slice_in_dim(
        padded_map, row_begin, block_rows + 2 * CONV_DILATION, 0
    )
    widened_columns = lax.dynamic_slice_in_dim(
        padded_map, column_begin, block_columns + 2 * CONV_DILATION, 0
    )
    row_keep = inside_mask(row_begin, block_rows, total_bins)
    col_keep = inside_mask(column_begin, block_columns, total_bins)
    widened_pair = (
        pair_features(widened_rows, widened_columns, width)
        * row_keep[:, None, None]
        * col_keep[None, None, :]
    )
    active = jnp.maximum(widened_pair, jnp.zeros((), jnp.bfloat16))
    base_offset = widened_pair[
        CONV_DILATION : CONV_DILATION + block_rows, :, CONV_DILATION : CONV_DILATION + block_columns
    ]
    half_sum = symmetric_conv(active, conv_kernel)
    result = (
        base_offset.astype(jnp.float32)
        + norm_gain[None, :, None] * half_sum
        + norm_bias[None, :, None]
    )
    return result.astype(jnp.bfloat16)


def solution(mesh):
    in_specs = (P("row", "col"), P("col", None), P(), P(), P())
    out_specs = P("row", None, "col")
    return jax.shard_map(
        per_device, mesh=mesh, in_specs=in_specs, out_specs=out_specs, check_vma=False
    )
```

profile of v0, /device:TPU:1, one launch (start us, length us, event | category | flops | bytes accessed | tf_op | source)
XLA Modules:
  0.0 331.6 jit_solution(3806741830517226296)
XLA Ops:
  6.5 0.0 copy-start
  6.5 0.0 all-gather.2.cloned.1.call-start
  6.5 0.7 copy-done
  7.2 0.9 fusion.32
  8.1 129.6 %all-reduce.2 = bf16[256,128]{1,0:T(8,128)(2,1)} all-reduce(f32[256,128]{1,0:T(8,128)S(1)} %fusion.32), channel_id=1, replica_groups=mesh['row'=16,'col'=32] {'col'}, use_global_device_ids=true, to_apply=%region_0.0 | all-reduce | flops 32768 | bytes 196608 | tf_op jit(solution)/shard_map/psum | solution.py:49
  137.7 0.0 all-gather.2.cloned.1.call-update
  137.7 1.0 copy.16
  138.8 1.1 copy.15
  139.8 0.1 slice.34
  139.9 0.1 slice.35
  140.0 0.7 broadcast_multiply_fusion
  140.6 86.0 %all-gather.2.cloned.1.call-done = bf16[4096,128]{1,0:T(8,128)(2,1)} async-done(((bf16[256,128]{1,0:T(8,128)(2,1)}), bf16[4096,128]{1,0:T(8,128)(2,1)}) %all-gather.2.cloned.1.call-update) | async-done | bytes 1048592 | tf_op jit(solution)/shard_map/all_gather | solution.py:50
  226.6 1.1 fusion.23
  227.7 0.1 copy.11
  227.8 0.1 copy.12
  228.0 0.9 convert_bitcast_fusion.1
  228.9 5.7 %fusion.19 = bf16[1,264,64,136]{1,2,3,0:T(8,128)(2,1)} fusion(f32[64,136]{0,1:T(8,128)S(1)} %get-tuple-element.8, f32[264,64]{0,1:T(8,128)S(1)} %copy.12, f32[64,136]{0,1:T(8,128)S(1)} %get-tuple-element.7, f32[264,64]{0,1:T(8,128)S(1)} %copy.11, bf16[136]{0:T(256)(128)(2,1)S(1)} %and_convert_fusion, bf16[264]{0:T(512)(128)(2,1)S(1)} %fusion.28), kind=kLoop, calls=%fused_computation.22 | loop fusion | flops 16084992 | bytes 4801312 | tf_op jit(solution)/shard_map/max | solution.py:65
  234.7 0.0 copy-start.3
  234.7 22.0 %copy.14 = bf16[264,64,1,8,17]{1,3,4,0,2:T(8,128)(2,1)} copy(bf16[264,64,1,8,17]{0,1,4,3,2:T(8,128)(2,1)} %bitcast.21) | data formatting | bytes 9191424 | tf_op jit(solution)/shard_map/conv_general_dilated | solution.py:29
  256.7 5.6 %slice.36 = bf16[264,64,1,7,8]{1,3,4,0,2:T(8,128)(2,1)} slice(bf16[264,64,1,8,17]{1,3,4,0,2:T(8,128)(2,1)} %copy.14), slice={[0:264], [0:64], [0:1], [1:8], [0:8]} | slice | bytes 3784704 | tf_op jit(solution)/shard_map/conv_general_dilated | solution.py:29
  262.3 0.0 copy-done.3
  262.3 19.8 %broadcast_select_fusion = f32[256,8,17,128]{3,1,2,0:T(8,128)} fusion(pred[8,17]{0,1:T(8,128)(4,1)S(1)} %copy-done.3, bf16[264,64,1,7,8]{1,3,4,0,2:T(8,128)(2,1)} %slice.36, bf16[264,64,1,8,17]{1,3,4,0,2:T(8,128)(2,1)} %copy.14, bf16[64,64,3,3]{0,1,3,2:T(8,128)(2,1)S(1)} %bitcast.24, bf16[64,64,3,3]{0,1,3,2:T(8,128)(2,1)S(1)} %bitcast.25), kind=kOutput, calls=%fused_computation.16 | convolution fusion | flops 5158854656 | bytes 24461448 | tf_op jit(solution)/shard_map/conv_general_dilated | solution.py:29
  282.1 14.9 %copy.17 = f32[256,8,17,128]{3,0,2,1:T(8,128)} copy(f32[256,8,17,128]{3,1,2,0:T(8,128)} %broadcast_select_fusion) | data formatting | bytes 35651584 | tf_op jit(solution)/shard_map/conv_general_dilated | solution.py:29
  297.0 0.0 copy-start.2
  297.0 6.9 %slice_bitcast_fusion = f32[256,128,128]{1,0,2:T(8,128)S(1)} fusion(f32[256,1,136,128]{3,0,2,1:T(8,128)} %bitcast.20), kind=kLoop, calls=%fused_computation.7 | loop fusion | bytes 33554432 | tf_op jit(solution)/shard_map/squeeze | solution.py:29
  303.9 0.0 copy-done.2
  303.9 0.0 copy-start.1
  303.9 9.2 %fusion.4 = bf16[256,64,128]{1,0,2:T(8,128)(2,1)} fusion(f32[256,128,128]{1,0,2:T(8,128)S(1)} %slice_bitcast_fusion, f32[64,128]{0,1:T(8,128)S(1)} %slice.33, f32[256,64]{1,0:T(8,128)S(1)} %slice.32, f32[64,128]{0,1:T(8,128)S(1)} %slice.31, f32[256,64]{1,0:T(8,128)S(1)} %slice.30, f32[64]{0:T(128)S(1)} %copy-done.2, f32[64]{0:T(128)S(1)} %broadcast_multiply_fusion, ...), kind=kLoop, calls=%fused_computation.6 | loop fusion | flops 25165824 | bytes 21169408 | tf_op jit(solution)/shard_map/convert_element_type | solution.py:75
  313.2 11.5 %copy.18 = bf16[256,64,128]{2,1,0:T(8,128)(2,1)} copy(bf16[256,64,128]{1,0,2:T(8,128)(2,1)} %fusion.4) | data formatting | bytes 8388608 | tf_op jit(solution)/shard_map/convert_element_type | solution.py:75
  324.7 0.0 copy-done.1
  (6 shorter events, 0.1 us)
Async XLA Ops:
  6.5 0.7 copy-start
  6.5 220.1 %all-gather.2.cloned.1.call-start = ((), (), s32[]{:S(2)}) async-start(), calls=%async_computation | async-start | bytes 1114112 | tf_op jit(solution)/shard_map/all_gather | solution.py:50
  234.7 27.7 %copy-start.3 = (pred[8,17]{0,1:T(8,128)(4,1)S(1)}, pred[8,17]{0,1:T(8,128)(4,1)}, u32[]{:S(2)}) copy-start(pred[8,17]{0,1:T(8,128)(4,1)} %constant.38) | copy-start | bytes 412
  297.0 6.9 %copy-start.2 = (f32[64]{0:T(128)S(1)}, f32[64]{0:T(128)}, u32[]{:S(2)}) copy-start(f32[64]{0:T(128)} %param.9) | copy-start | bytes 772
  303.9 20.8 %copy-start.1 = (bf16[256,16]{0,1:T(8,128)(2,1)S(1)}, bf16[256,16]{0,1:T(8,128)(2,1)}, u32[]{:S(2)}) copy-start(bf16[256,16]{0,1:T(8,128)(2,1)} %param.5) | copy-start | bytes 24580
Sparse Core Ops, SparseCore 0:
  137.8 88.7 all-gather.1
where the time goes:
time: 332 us
  blocking collectives  130 us (39%)
  waiting for transfers between devices  86 us (26%)
  local copies, waits for them, and re-layouts  64.2 us (19%)
  matrix products  20.6 us (6%)
  other arithmetic  17.7 us (5%)
  between operations  13.5 us (4%)
    psum x1, blocking collectives, per_device(): summed = lax.psum(partial_sum, 'col').astype(jnp.bfloat16)  130 us
    all_gather x1, waiting for transfers between devices, per_device(): feature_rows = lax.all_gather(summed, 'row', axis=0, tiled=True)  86 us
    conv_general_dilated x3, local copies, waits for them, and re-layouts, symmetric_conv(): lax.conv_general_dilated(active[None], stacked, (1, 1), 'VALID', rhs_dila...  42.5 us
    conv_general_dilated x1, matrix products, symmetric_conv(): lax.conv_general_dilated(active[None], stacked, (1, 1), 'VALID', rhs_dila...  19.8 us
    convert_element_type x1, local copies, waits for them, and re-layouts, per_device(): return result.astype(jnp.bfloat16)  11.5 us
    convert_element_type x1, other arithmetic, per_device(): return result.astype(jnp.bfloat16)  9.23 us
    squeeze x1, local copies, waits for them, and re-layouts, symmetric_conv(): lax.conv_general_dilated(active[None], stacked, (1, 1), 'VALID', rhs_dila...  6.93 us
  transfers between devices with their start and end apart: 1, of which 1 were waited for; matrix products, arithmetic and copies ran while one was open for 1% of the time, Pallas kernels for 0%

commit v1 on v0

--- a/solution.py
+++ b/solution.py
@@ -46,7 +46,7 @@
     row_begin = lax.axis_index("row") * block_rows
     column_begin = lax.axis_index("col") * block_columns
     partial_sum = jnp.dot(trunk, proj_weight, preferred_element_type=jnp.float32)
-    summed = lax.psum(partial_sum, "col").astype(jnp.bfloat16)
+    summed = jnp.sum(lax.all_gather(partial_sum, "col"), axis=0).astype(jnp.bfloat16)
     feature_rows = lax.all_gather(summed, "row", axis=0, tiled=True)
     padded_map = jnp.pad(feature_rows, ((CONV_DILATION, CONV_DILATION), (0, 0)))
     widened_rows = lax.dynamic_slice_in_dim(

time: 332 us -> 347 us (1.045)
  waiting for transfers between devices: 86 us -> 226 us
  blocking collectives: 130 us -> 0 us
    all_gather x0 -> x1, waiting for transfers between devices: none -> 145 us  [per_device(): lax.all_gather(partial_sum, 'col')]
    psum x1 -> x0, blocking collectives: 130 us -> none  [per_device(): summed = lax.psum(partial_sum, 'col').astype(jnp.bfloat16)]
    all_gather x1, waiting for transfers between devices: 86 us -> 80.9 us  [per_device(): feature_rows = lax.all_gather(summed, 'row', axis=0, tiled=True)]
  transfers between devices with their start and end apart: 1 -> 2, of which waited for: 1 -> 2; matrix products, arithmetic and copies ran while one was open for 1% -> 1% of each run, Pallas kernels for 0% -> 0%
where the time goes in v1:
time: 347 us; the launch traced here: 346 us
  waiting for transfers between devices  226 us (65%)
  local copies, waits for them, and re-layouts  64.2 us (19%)
  matrix products  21.3 us (6%)
  other arithmetic  20.7 us (6%)
  between operations  13.5 us (4%)
    all_gather x1, waiting for transfers between devices, per_device(): lax.all_gather(partial_sum, 'col')  145 us
    all_gather x1, waiting for transfers between devices, per_device(): feature_rows = lax.all_gather(summed, 'row', axis=0, tiled=True)  80.9 us
    conv_general_dilated x3, local copies, waits for them, and re-layouts, symmetric_conv(): lax.conv_general_dilated(active[None], stacked, (1, 1), 'VALID', rhs_dila...  42.5 us
    conv_general_dilated x1, matrix products, symmetric_conv(): lax.conv_general_dilated(active[None], stacked, (1, 1), 'VALID', rhs_dila...  19.7 us
    convert_element_type x1, local copies, waits for them, and re-layouts, per_device(): return result.astype(jnp.bfloat16)  11.5 us
    convert_element_type x1, other arithmetic, per_device(): return result.astype(jnp.bfloat16)  9.23 us
  transfers between devices with their start and end apart: 2, of which 2 were waited for; matrix products, arithmetic and copies ran while one was open for 1% of the time, Pallas kernels for 0%

profile of v1, /device:TPU:1, one launch (start us, length us, event | category | flops | bytes accessed | tf_op | source)
XLA Modules:
  0.0 345.9 jit_solution(15805873476978365967)
XLA Ops:
  6.5 0.0 copy-start
  6.5 0.0 all-gather.6.cloned.1.call-start
  6.5 0.7 copy-done
  7.2 1.5 fusion.32
  8.8 0.0 all-gather.6.cloned.1.call-update
  8.8 0.0 all-gather.4.cloned.1.call-start
  8.9 145.2 %all-gather.6.cloned.1.call-done = f32[8192,128]{1,0:T(8,128)} async-done(((f32[256,128]{1,0:T(8,128)}), f32[8192,128]{1,0:T(8,128)}) %all-gather.6.cloned.1.call-update) | async-done | bytes 4194320 | tf_op jit(solution)/shard_map/all_gather | solution.py:49
  154.1 3.0 reduce_sum.9
  157.1 0.0 all-gather.4.cloned.1.call-update
  157.1 1.0 copy.16
  158.2 1.1 copy.15
  159.2 0.1 slice.34
  159.3 0.1 slice.35
  159.4 0.7 broadcast_multiply_fusion
  160.1 80.9 %all-gather.4.cloned.1.call-done = bf16[4096,128]{1,0:T(8,128)(2,1)} async-done(((bf16[256,128]{1,0:T(8,128)(2,1)}), bf16[4096,128]{1,0:T(8,128)(2,1)}) %all-gather.4.cloned.1.call-update) | async-done | bytes 1048592 | tf_op jit(solution)/shard_map/all_gather | solution.py:50
  241.0 1.1 fusion.23
  242.0 0.1 copy.11
  242.2 0.1 copy.12
  242.3 0.9 convert_bitcast_fusion.1
  243.3 5.8 %fusion.19 = bf16[1,264,64,136]{1,2,3,0:T(8,128)(2,1)} fusion(f32[64,136]{0,1:T(8,128)S(1)} %get-tuple-element.8, f32[264,64]{0,1:T(8,128)S(1)} %copy.12, f32[64,136]{0,1:T(8,128)S(1)} %get-tuple-element.7, f32[264,64]{0,1:T(8,128)S(1)} %copy.11, bf16[136]{0:T(256)(128)(2,1)S(1)} %and_convert_fusion, bf16[264]{0:T(512)(128)(2,1)S(1)} %fusion.28), kind=kLoop, calls=%fused_computation.22 | loop fusion | flops 16084992 | bytes 4801312 | tf_op jit(solution)/shard_map/max | solution.py:65
  249.1 0.0 copy-start.3
  249.1 22.0 %copy.14 = bf16[264,64,1,8,17]{1,3,4,0,2:T(8,128)(2,1)} copy(bf16[264,64,1,8,17]{0,1,4,3,2:T(8,128)(2,1)} %bitcast.22) | data formatting | bytes 9191424 | tf_op jit(solution)/shard_map/conv_general_dilated | solution.py:29
  271.1 5.6 %slice.36 = bf16[264,64,1,7,8]{1,3,4,0,2:T(8,128)(2,1)} slice(bf16[264,64,1,8,17]{1,3,4,0,2:T(8,128)(2,1)} %copy.14), slice={[0:264], [0:64], [0:1], [1:8], [0:8]} | slice | bytes 3784704 | tf_op jit(solution)/shard_map/conv_general_dilated | solution.py:29
  276.7 0.0 copy-done.3
  276.7 19.7 %broadcast_select_fusion = f32[256,8,17,128]{3,1,2,0:T(8,128)} fusion(pred[8,17]{0,1:T(8,128)(4,1)S(1)} %copy-done.3, bf16[264,64,1,7,8]{1,3,4,0,2:T(8,128)(2,1)} %slice.36, bf16[264,64,1,8,17]{1,3,4,0,2:T(8,128)(2,1)} %copy.14, bf16[64,64,3,3]{0,1,3,2:T(8,128)(2,1)S(1)} %bitcast.26, bf16[64,64,3,3]{0,1,3,2:T(8,128)(2,1)S(1)} %bitcast.27), kind=kOutput, calls=%fused_computation.16 | convolution fusion | flops 5158854656 | bytes 24461448 | tf_op jit(solution)/shard_map/conv_general_dilated | solution.py:29
  296.5 14.8 %copy.17 = f32[256,8,17,128]{3,0,2,1:T(8,128)} copy(f32[256,8,17,128]{3,1,2,0:T(8,128)} %broadcast_select_fusion) | data formatting | bytes 35651584 | tf_op jit(solution)/shard_map/conv_general_dilated | solution.py:29
  311.3 6.9 %slice_bitcast_fusion = f32[256,128,128]{1,0,2:T(8,128)S(1)} fusion(f32[256,1,136,128]{3,0,2,1:T(8,128)} %bitcast.21), kind=kLoop, calls=%fused_computation.7 | loop fusion | bytes 33554432 | tf_op jit(solution)/shard_map/squeeze | solution.py:29
  318.2 0.0 copy-done.2
  318.2 0.0 copy-start.1
  318.2 9.2 %fusion.4 = bf16[256,64,128]{1,0,2:T(8,128)(2,1)} fusion(f32[256,128,128]{1,0,2:T(8,128)S(1)} %slice_bitcast_fusion, f32[64,128]{0,1:T(8,128)S(1)} %slice.33, f32[256,64]{1,0:T(8,128)S(1)} %slice.32, f32[64,128]{0,1:T(8,128)S(1)} %slice.31, f32[256,64]{1,0:T(8,128)S(1)} %slice.30, f32[64]{0:T(128)S(1)} %copy-done.2, f32[64]{0:T(128)S(1)} %broadcast_multiply_fusion, ...), kind=kLoop, calls=%fused_computation.6 | loop fusion | flops 25165824 | bytes 21169408 | tf_op jit(solution)/shard_map/convert_element_type | solution.py:75
  327.5 11.5 %copy.18 = bf16[256,64,128]{2,1,0:T(8,128)(2,1)} copy(bf16[256,64,128]{1,0,2:T(8,128)(2,1)} %fusion.4) | data formatting | bytes 8388608 | tf_op jit(solution)/shard_map/convert_element_type | solution.py:75
  339.0 0.0 copy-done.1
  (7 shorter events, 0.1 us)
Async XLA Ops:
  6.5 0.7 copy-start
  6.5 147.5 %all-gather.6.cloned.1.call-start = ((), (), s32[]{:S(2)}) async-start(), calls=%async_computation.1 | async-start | bytes 4325376 | tf_op jit(solution)/shard_map/all_gather | solution.py:49
  8.8 232.2 %all-gather.4.cloned.1.call-start = ((), (), s32[]{:S(2)}) async-start(), calls=%async_computation | async-start | bytes 1114112 | tf_op jit(solution)/shard_map/all_gather | solution.py:50
  249.1 27.7 %copy-start.3 = (pred[8,17]{0,1:T(8,128)(4,1)S(1)}, pred[8,17]{0,1:T(8,128)(4,1)}, u32[]{:S(2)}) copy-start(pred[8,17]{0,1:T(8,128)(4,1)} %constant.40) | copy-start | bytes 412
  311.3 6.9 %copy-start.2 = (f32[64]{0:T(128)S(1)}, f32[64]{0:T(128)}, u32[]{:S(2)}) copy-start(f32[64]{0:T(128)} %param.9) | copy-start | bytes 772
  318.2 20.8 %copy-start.1 = (bf16[256,16]{0,1:T(8,128)(2,1)S(1)}, bf16[256,16]{0,1:T(8,128)(2,1)}, u32[]{:S(2)}) copy-start(bf16[256,16]{0,1:T(8,128)(2,1)} %param.5) | copy-start | bytes 24580
Sparse Core Ops, SparseCore 0:
  9.4 144.5 all-gather.5
  157.4 83.5 all-gather.3
